TPU v7x, 32 devices: a whole 2x2x4 slice. The times are simulated.
32 devices in a mesh: groups: 2 (over y), seq: 4 (over z), adapt: 4 (over x, core).
Axes of the slice: x: 2, y: 2, z: 4, core: 2. Of those that a mesh axis runs over, the one named last changes fastest.
Arguments:
- image: bfloat16 [16, 2048, 3072], P(('groups', 'adapt'), 'seq'), parts along dimension 0, may hold values from -6 to 6
- modulation: float32 [16, 2, 3072], P(('groups', 'adapt')), parts along dimension 0, may hold values from -3 to 3
- query_key_value_weight: bfloat16 [3072, 6144], P(None, 'adapt'), may hold values from -0.109375 to 0.109375
- pooled_down_factor: bfloat16 [16, 3072, 64], P('seq'), may hold values from -0.109375 to 0.109375
- pooled_up_factor: bfloat16 [16, 64, 6144], P('seq', None, 'adapt'), may hold values from -0.75 to 0.75
- request_adapter: int32 [16], P('groups'), parts along dimension 0, may hold values from 0 to 15
- adapter_slot_table: int32 [16], replicated, may hold values from 0 to 15, each once
- row_request: int32 [16], P('groups'), parts along dimension 0, may hold values from 0 to 7, each once
- text_key_value: bfloat16 [16, 512, 2, 2048], P('groups', 'seq', None, 'adapt'), parts along dimension 0, may hold values from -110 to 110
- query_key_gain: float32 [2, 128], replicated, may hold values from 1 to 2.5
Outputs:
- attended: bfloat16 [16, 2048, 2048], P('groups', 'seq', 'adapt'), parts along dimension 0
There are 2 independent parts, one for each index of `groups`. A program takes and returns all parts, laid end to end along the dimension named above; an argument that names none is the same for every part. Nothing has to cross between parts.
All inputs are finite; a program needn't handle non-finite values.
Results may differ from a plain program's by a relative error of at most 0.0049.
The roundings to bfloat16 on the way count: a program that leaves them out, or rounds other values in their place, can miss the bound.
Values may be sent and summed in bfloat16 or wider, within the bound.
A program may use at most 192 MiB of HBM per device.

v0:
```python
import math
import jax
import jax.numpy as jnp
from jax import lax
from jax.sharding import PartitionSpec as P

HEAD_SIZE = 128


def layer_modulate(image, modulation):
    widened = image.astype(jnp.float32)
    centre = widened - jnp.mean(widened, axis=-1, keepdims=True)
    variance = jnp.mean(centre * centre, axis=-1, keepdims=True)
    normed = centre * lax.rsqrt(variance + 1e-06)
    return ((1.0 + modulation[:, 1, None, :]) * normed + modulation[:, 0, None, :]).astype(
        jnp.bfloat16
    )


def rms_scale(values, gain):
    return values * lax.rsqrt(jnp.mean(values * values, axis=-1, keepdims=True) + 1e-06) * gain


def attend_item(operands):
    queries, joined = operands
    key_rows = joined[:, 0]
    value_rows = joined[:, 1]
    query_count = queries.shape[0]
    block = math.gcd(query_count, 512)
    inverse = 1.0 / math.sqrt(queries.shape[-1])
    blocked = queries.reshape(query_count // block, block, queries.shape[-1])

    def one_block(block_rows):
        scores = (
            lax.dot_general(
                block_rows, key_rows, (((1,), (1,)), ((), ())), preferred_element_type=jnp.float32
            )
            * inverse
        )
        highest = jnp.max(scores, axis=-1, keepdims=True)
        weights = jnp.exp(scores - highest)
        weights = weights / jnp.sum(weights, axis=-1, keepdims=True)
        return jnp.dot(
            weights.astype(jnp.bfloat16), value_rows, preferred_element_type=jnp.float32
        ).astype(jnp.bfloat16)

    return lax.map(one_block, blocked).reshape(queries.shape)


def on_device(
    image,
    modulation,
    query_key_value_weight,
    pooled_down_factor,
    pooled_up_factor,
    request_adapter,
    adapter_slot_table,
    row_request,
    text_key_value,
    query_key_gain,
):
    seq_index = lax.axis_index("seq")
    all_requests = request_adapter.shape[0]
    local_pool_slice = pooled_down_factor.shape[0]
    pool_total = adapter_slot_table.shape[0]
    heads_local = query_key_value_weight.shape[1] // (3 * HEAD_SIZE)
    text_local = text_key_value.shape[1]
    modulated = layer_modulate(image, modulation)
    request_match = row_request[:, None] == jnp.arange(all_requests, dtype=jnp.int32)[None, :]
    chosen_ids = jnp.sum(jnp.where(request_match, request_adapter[None, :], 0), axis=1)
    slot_match = chosen_ids[:, None] == jnp.arange(pool_total, dtype=jnp.int32)[None, :]
    slots = jnp.sum(jnp.where(slot_match, adapter_slot_table[None, :], 0), axis=1)
    owned = slots // local_pool_slice == seq_index
    local_match = (slots % local_pool_slice)[:, None] == jnp.arange(
        local_pool_slice, dtype=jnp.int32
    )[None, :]
    slot_picker = (owned[:, None] & local_match).astype(jnp.bfloat16)
    up_terms = jnp.einsum(
        "eq,qfx->efx", slot_picker, pooled_up_factor, preferred_element_type=jnp.float32
    ).astype(jnp.bfloat16)
    down_terms = jnp.einsum(
        "mv,vna->mna", slot_picker, pooled_down_factor, preferred_element_type=jnp.float32
    ).astype(jnp.bfloat16)
    down_fetched, up_fetched = (
        lax.psum(down_terms, "seq").astype(jnp.float32),
        lax.psum(up_terms, "seq").astype(jnp.float32),
    )
    down_fetched = down_fetched.astype(jnp.bfloat16)
    up_fetched = up_fetched.astype(jnp.bfloat16)
    block_rows = lax.all_gather(modulated, "adapt", axis=0, tiled=True)
    shrunk = jnp.einsum(
        "rtd,rdk->rtk", block_rows, down_fetched, preferred_element_type=jnp.float32
    ).astype(jnp.bfloat16)
    frozen = jnp.einsum(
        "rtd,dc->rtc", block_rows, query_key_value_weight, preferred_element_type=jnp.float32
    )
    qkv = frozen + jnp.einsum(
        "rtk,rkc->rtc", shrunk, up_fetched, preferred_element_type=jnp.float32
    )
    token_local = qkv.shape[1]
    qkv = qkv.reshape(all_requests, token_local, heads_local, 3, HEAD_SIZE)
    queries = rms_scale(qkv[:, :, :, 0], query_key_gain[0]).astype(jnp.bfloat16)
    image_keys = rms_scale(qkv[:, :, :, 1], query_key_gain[1]).astype(jnp.bfloat16)
    image_values = qkv[:, :, :, 2].astype(jnp.bfloat16)
    image_pairs = jnp.transpose(jnp.stack([image_keys, image_values], axis=3), (0, 2, 1, 3, 4))
    text_pairs = jnp.transpose(
        text_key_value.reshape(all_requests, text_local, 2, heads_local, HEAD_SIZE), (0, 3, 1, 2, 4)
    )
    joined = jnp.concatenate([image_pairs, text_pairs], axis=2)
    joined = joined.reshape(all_requests * heads_local, token_local + text_local, 2, HEAD_SIZE)
    queries = jnp.transpose(queries, (0, 2, 1, 3)).reshape(
        all_requests * heads_local, token_local, HEAD_SIZE
    )
    query_items, joined_items = (
        lax.all_to_all(queries, "seq", split_axis=0, concat_axis=1, tiled=True),
        lax.all_to_all(joined, "seq", split_axis=0, concat_axis=1, tiled=True),
    )
    attended = lax.map(attend_item, (query_items, joined_items))
    returned = lax.all_to_all(attended, "seq", split_axis=1, concat_axis=0, tiled=True)
    returned = returned.reshape(all_requests, heads_local, token_local, HEAD_SIZE)
    return jnp.transpose(returned, (0, 2, 1, 3)).reshape(
        all_requests, token_local, heads_local * HEAD_SIZE
    )


def solution(mesh):
    in_specs = (
        P(("groups", "adapt"), "seq", None),
        P(("groups", "adapt"), None, None),
        P(None, "adapt"),
        P("seq", None, None),
        P("seq", None, "adapt"),
        P("groups"),
        P(),
        P("groups"),
        P("groups", "seq", None, "adapt"),
        P(),
    )
    out_specs = P("groups", "seq", "adapt")
    return jax.shard_map(
        on_device, mesh=mesh, in_specs=in_specs, out_specs=out_specs, check_vma=False
    )
```

profile of v0, /device:TPU:0, one launch (start us, length us, event | category | flops | bytes accessed | tf_op | source)
XLA Modules:
  0.0 888.3 jit_solution(3175267230559958143)
XLA Ops:
  9.2 2.8 convolution_convert_fusion
  12.1 3.1 convolution_convert_fusion.1
  15.2 3.7 convert_reduce_fusion
  18.9 4.5 fusion.10
  23.6 9.4 %fusion.13 = bf16[2,512,3072]{2,1,0:T(8,128)(2,1)} fusion(bf16[2,512,3072]{2,1,0:T(8,128)(2,1)} %param.14, f32[2,3072]{1,0:T(2,128)S(1)} %get-tuple-element.83, f32[2,512]{1,0:T(2,128)S(1)} %add_rsqrt_fusion.2, f32[2,512]{1,0:T(2,128)S(1)} %broadcast_multiply_fusion, f32[2,3072]{1,0:T(2,128)S(1)} %get-tuple-element.84), kind=kLoop, calls=%fused_computation.24 | loop fusion | flops 18874368 | bytes 12640256 | tf_op jit(solution)/shard_map/convert_element_type | solution.py:15
  34.2 156.1 %all-reduce.3.cloned.1.call-done = (bf16[8,64,1536]{2,0,1:T(8,128)(2,1)}, bf16[8,3072,64]{1,0,2:T(8,128)(2,1)}) async-done(((bf16[8,64,1536]{2,0,1:T(8,128)(2,1)}, bf16[8,3072,64]{1,0,2:T(8,128)(2,1)}), (bf16[8,64,1536]{2,0,1:T(8,128)(2,1)}, bf16[8,3072,64]{1,0,2:T(8,128)(2,1)})) %all-reduce.3.cloned.1.call-update) | async-done | bytes 4718608 | tf_op jit(solution)/shard_map/psum | solution.py:86
  190.3 23.9 %fusion.18 = f32[8,512,1536]{2,1,0:T(8,128)} fusion(bf16[8,64,1536]{2,0,1:T(8,128)(2,1)} %get-tuple-element.73, bf16[8,512,3072]{2,1,0:T(8,128)(2,1)} %all-gather.2.cloned.1.call-done, bf16[8,3072,64]{1,0,2:T(8,128)(2,1)} %get-tuple-element.74), kind=kOutput, calls=%fused_computation.40 | convolution fusion | flops 2416181248 | bytes 55050240 | tf_op jit(solution)/shard_map/rtk,rkc->rtc/dot_general | solution.py:97
  214.3 47.6 %convolution_add_fusion = f32[8,512,1536]{2,1,0:T(8,128)} fusion(f32[8,512,1536]{2,1,0:T(8,128)} %fusion.18, bf16[8,512,3072]{2,1,0:T(8,128)(2,1)} %all-gather.2.cloned.1.call-done, bf16[3072,1536]{1,0:T(8,128)(2,1)} %param.16), kind=kOutput, calls=%fused_computation.16 | convolution fusion | flops 38660997120 | bytes 84934656 | tf_op jit(solution)/shard_map/rtd,dc->rtc/dot_general | solution.py:94
  261.9 24.7 %copy.49 = f32[8,512,1536]{1,2,0:T(8,128)} copy(f32[8,512,1536]{2,1,0:T(8,128)} %convolution_add_fusion) | data formatting | bytes 50331648 | tf_op jit(solution)/shard_map/add | solution.py:97
  286.6 4.6 multiply_reduce_fusion.1
  291.2 7.0 fusion.15
  298.2 6.5 copy.50
  304.6 5.2 all-to-all-start
  309.8 6.2 copy.52
  316.0 3.2 copy.79
  319.1 4.0 slice.55
  323.1 4.6 multiply_reduce_fusion
  327.8 7.0 multiply_convert_fusion
  334.7 6.2 maximum_bitcast_fusion
  340.9 9.1 %pad_maximum_fusion = bf16[8,4,640,2,128]{2,4,3,1,0:T(8,128)(2,1)} fusion(bf16[8,4,128,2,128]{2,4,3,1,0:T(8,128)(2,1)} %bitcast.102, bf16[8,4,512,2,128]{2,4,3,1,0:T(8,128)(2,1)} %maximum_bitcast_fusion), kind=kLoop, calls=%fused_computation.25 | loop fusion | flops 20971520 | bytes 20971520 | tf_op jit(solution)/shard_map/concatenate | solution.py:109
  350.1 15.1 %copy.54 = bf16[8,4,640,2,128]{4,2,3,1,0:T(8,128)(2,1)} copy(bf16[8,4,640,2,128]{2,4,3,1,0:T(8,128)(2,1)} %pad_maximum_fusion) | data formatting | bytes 20971520 | tf_op jit(solution)/shard_map/concatenate | solution.py:109
  365.2 38.2 %all-to-all-done = bf16[32,512,128]{2,1,0:T(8,128)(2,1)} async-done(((bf16[32,512,128]{2,1,0:T(8,128)(2,1)}), bf16[32,512,128]{2,1,0:T(8,128)(2,1)}, u32[]{:S(2)}, u32[]{:S(2)}) %all-to-all-start) | async-done | bytes 4194336 | tf_op jit(solution)/shard_map/all_to_all | solution.py:115
  403.3 6.0 all-to-all-start.1
  409.4 4.6 copy.51
  414.0 223.2 %all-to-all-done.1 = bf16[32,640,2,128]{3,1,2,0:T(8,128)(2,1)} async-done(((bf16[32,640,2,128]{3,1,2,0:T(8,128)(2,1)}), bf16[32,640,2,128]{3,1,2,0:T(8,128)(2,1)}, u32[]{:S(2)}, u32[]{:S(2)}) %all-to-all-start.1) | async-done | bytes 10485792 | tf_op jit(solution)/shard_map/all_to_all | solution.py:116
  637.1 9.2 %copy.55 = bf16[8,4,640,2,128]{4,2,1,3,0:T(8,128)(2,1)} copy(bf16[8,4,640,2,128]{4,2,3,0,1:T(8,128)(2,1)} %bitcast.23) | data formatting | bytes 20971520 | tf_op jit(solution)/shard_map/all_to_all | solution.py:116
  646.3 118.3 %while.21 = (s32[]{:T(128)}, bf16[8,2048,128]{2,1,0:T(8,128)(2,1)}, bf16[8,2048,128]{2,1,0:T(8,128)(2,1)}, bf16[8,2560,2,128]{3,1,2,0:T(8,128)(2,1)}, s32[]{:T(128)}, /*index=5*/s32[]{:T(128)}, s32[]{:T(128)}) while((s32[]{:T(128)}, bf16[8,2048,128]{2,1,0:T(8,128)(2,1)}, bf16[8,2048,128]{2,1,0:T(8,128)(2,1)}, ...), condition=%wide.region_13.14_spmd, body=%wide.region_8.13_spmd.sunk | while | flops 680328192 | bytes 24652504 | solution.py:118
  646.3 1.4 dynamic-slice_bitcast_fusion.2
  648.9 11.3 %while.22 = (s32[]{:T(128)}, bf16[4,512,128]{2,1,0:T(8,128)(2,1)S(1)}, bf16[4,512,128]{2,1,0:T(8,128)(2,1)S(1)}, bf16[2560,128]{1,0:T(8,128)(2,1)S(1)}, bf16[2560,128]{1,0:T(8,128)(2,1)S(1)}, /*index=5*/s32[]{:T(128)}) while((s32[]{:T(128)}, bf16[4,512,128]{2,1,0:T(8,128)(2,1)S(1)}, bf16[4,512,128]{2,1,0:T(8,128)(2,1)S(1)}, ...), condition=%wide.region_12.12_spmd, body=%wide.region_9.11_spmd.sunk | while | flops 680328192 | bytes 17311820 | solution.py:47
  661.1 1.4 dynamic-slice_bitcast_fusion.2
  663.7 11.4 %while.22 = (s32[]{:T(128)}, bf16[4,512,128]{2,1,0:T(8,128)(2,1)S(1)}, bf16[4,512,128]{2,1,0:T(8,128)(2,1)S(1)}, bf16[2560,128]{1,0:T(8,128)(2,1)S(1)}, bf16[2560,128]{1,0:T(8,128)(2,1)S(1)}, /*index=5*/s32[]{:T(128)}) while((s32[]{:T(128)}, bf16[4,512,128]{2,1,0:T(8,128)(2,1)S(1)}, bf16[4,512,128]{2,1,0:T(8,128)(2,1)S(1)}, ...), condition=%wide.region_12.12_spmd, body=%wide.region_9.11_spmd.sunk | while | flops 680328192 | bytes 17311820 | solution.py:47
  675.9 1.4 dynamic-slice_bitcast_fusion.2
  678.5 11.4 %while.22 = (s32[]{:T(128)}, bf16[4,512,128]{2,1,0:T(8,128)(2,1)S(1)}, bf16[4,512,128]{2,1,0:T(8,128)(2,1)S(1)}, bf16[2560,128]{1,0:T(8,128)(2,1)S(1)}, bf16[2560,128]{1,0:T(8,128)(2,1)S(1)}, /*index=5*/s32[]{:T(128)}) while((s32[]{:T(128)}, bf16[4,512,128]{2,1,0:T(8,128)(2,1)S(1)}, bf16[4,512,128]{2,1,0:T(8,128)(2,1)S(1)}, ...), condition=%wide.region_12.12_spmd, body=%wide.region_9.11_spmd.sunk | while | flops 680328192 | bytes 17311820 | solution.py:47
  690.7 1.4 dynamic-slice_bitcast_fusion.2
  693.3 11.4 %while.22 = (s32[]{:T(128)}, bf16[4,512,128]{2,1,0:T(8,128)(2,1)S(1)}, bf16[4,512,128]{2,1,0:T(8,128)(2,1)S(1)}, bf16[2560,128]{1,0:T(8,128)(2,1)S(1)}, bf16[2560,128]{1,0:T(8,128)(2,1)S(1)}, /*index=5*/s32[]{:T(128)}) while((s32[]{:T(128)}, bf16[4,512,128]{2,1,0:T(8,128)(2,1)S(1)}, bf16[4,512,128]{2,1,0:T(8,128)(2,1)S(1)}, ...), condition=%wide.region_12.12_spmd, body=%wide.region_9.11_spmd.sunk | while | flops 680328192 | bytes 17311820 | solution.py:47
  705.5 1.4 dynamic-slice_bitcast_fusion.2
  708.1 11.4 %while.22 = (s32[]{:T(128)}, bf16[4,512,128]{2,1,0:T(8,128)(2,1)S(1)}, bf16[4,512,128]{2,1,0:T(8,128)(2,1)S(1)}, bf16[2560,128]{1,0:T(8,128)(2,1)S(1)}, bf16[2560,128]{1,0:T(8,128)(2,1)S(1)}, /*index=5*/s32[]{:T(128)}) while((s32[]{:T(128)}, bf16[4,512,128]{2,1,0:T(8,128)(2,1)S(1)}, bf16[4,512,128]{2,1,0:T(8,128)(2,1)S(1)}, ...), condition=%wide.region_12.12_spmd, body=%wide.region_9.11_spmd.sunk | while | flops 680328192 | bytes 17311820 | solution.py:47
  720.3 1.4 dynamic-slice_bitcast_fusion.2
  722.9 11.4 %while.22 = (s32[]{:T(128)}, bf16[4,512,128]{2,1,0:T(8,128)(2,1)S(1)}, bf16[4,512,128]{2,1,0:T(8,128)(2,1)S(1)}, bf16[2560,128]{1,0:T(8,128)(2,1)S(1)}, bf16[2560,128]{1,0:T(8,128)(2,1)S(1)}, /*index=5*/s32[]{:T(128)}) while((s32[]{:T(128)}, bf16[4,512,128]{2,1,0:T(8,128)(2,1)S(1)}, bf16[4,512,128]{2,1,0:T(8,128)(2,1)S(1)}, ...), condition=%wide.region_12.12_spmd, body=%wide.region_9.11_spmd.sunk | while | flops 680328192 | bytes 17311820 | solution.py:47
  735.1 1.4 dynamic-slice_bitcast_fusion.2
  737.6 11.4 %while.22 = (s32[]{:T(128)}, bf16[4,512,128]{2,1,0:T(8,128)(2,1)S(1)}, bf16[4,512,128]{2,1,0:T(8,128)(2,1)S(1)}, bf16[2560,128]{1,0:T(8,128)(2,1)S(1)}, bf16[2560,128]{1,0:T(8,128)(2,1)S(1)}, /*index=5*/s32[]{:T(128)}) while((s32[]{:T(128)}, bf16[4,512,128]{2,1,0:T(8,128)(2,1)S(1)}, bf16[4,512,128]{2,1,0:T(8,128)(2,1)S(1)}, ...), condition=%wide.region_12.12_spmd, body=%wide.region_9.11_spmd.sunk | while | flops 680328192 | bytes 17311820 | solution.py:47
  749.8 1.4 dynamic-slice_bitcast_fusion.2
  752.4 11.4 %while.22 = (s32[]{:T(128)}, bf16[4,512,128]{2,1,0:T(8,128)(2,1)S(1)}, bf16[4,512,128]{2,1,0:T(8,128)(2,1)S(1)}, bf16[2560,128]{1,0:T(8,128)(2,1)S(1)}, bf16[2560,128]{1,0:T(8,128)(2,1)S(1)}, /*index=5*/s32[]{:T(128)}) while((s32[]{:T(128)}, bf16[4,512,128]{2,1,0:T(8,128)(2,1)S(1)}, bf16[4,512,128]{2,1,0:T(8,128)(2,1)S(1)}, ...), condition=%wide.region_12.12_spmd, body=%wide.region_9.11_spmd.sunk | while | flops 680328192 | bytes 17311820 | solution.py:47
  764.6 4.9 copy.56
  769.5 95.4 %all_to_all.51 = bf16[8,2048,128]{2,0,1:T(8,128)(2,1)S(1)} all-to-all(bf16[8,2048,128]{2,0,1:T(8,128)(2,1)S(1)} %copy.56), channel_id=1, replica_groups=mesh['groups'=2,'seq'=4,'adapt'=4] {'seq'}, dimensions={1} | all-to-all | bytes 8388608 | tf_op jit(solution)/shard_map/all_to_all | solution.py:119
  864.9 2.9 copy.58
  867.8 6.6 copy.59
  874.4 6.4 copy.60
  (155 shorter events, 109.5 us)
Async XLA Ops:
  7.4 1.8 copy-start
  7.4 182.9 %all-reduce.3.cloned.1.call-start = ((), (), s32[]{:S(2)}) async-start(), calls=%async_computation.4 | async-start | bytes 9437184 | tf_op jit(solution)/shard_map/psum | solution.py:86
  15.2 8.3 copy-start.2
  15.2 175.1 %all-gather.2.cloned.1.call-start = ((), (), s32[]{:S(2)}) async-start(), calls=%async_computation.3 | async-start | bytes 31457280 | tf_op jit(solution)/shard_map/all_gather | solution.py:90
  33.0 0.7 copy-start.4
  304.6 98.7 %all-to-all-start = ((bf16[32,512,128]{2,1,0:T(8,128)(2,1)}), bf16[32,512,128]{2,1,0:T(8,128)(2,1)}, u32[]{:S(2)}, u32[]{:S(2)}) async-start(bf16[32,512,128]{2,1,0:T(8,128)(2,1)} %bitcast.96), calls=%async_computation | async-start | bytes 8388608 | tf_op jit(solution)/shard_map/all_to_all | solution.py:115
  323.1 4.6 copy-start.3
  403.3 233.8 %all-to-all-start.1 = ((bf16[32,640,2,128]{3,1,2,0:T(8,128)(2,1)}), bf16[32,640,2,128]{3,1,2,0:T(8,128)(2,1)}, u32[]{:S(2)}, u32[]{:S(2)}) async-start(bf16[32,640,2,128]{3,1,2,0:T(8,128)(2,1)} %bitcast.94), calls=%async_computation.1 | async-start | bytes 20971520 | tf_op jit(solution)/shard_map/all_to_all | solution.py:116
  867.8 13.0 %copy-start.1 = (bf16[4,3072,64]{1,2,0:T(8,128)(2,1)S(1)}, bf16[4,3072,64]{1,2,0:T(8,128)(2,1)}, u32[]{:S(2)}) copy-start(bf16[4,3072,64]{1,2,0:T(8,128)(2,1)} %param.17) | copy-start | bytes 4718596
Sparse Core Ops, SparseCore 0:
  15.3 174.9 all-reduce.2
Sparse Core Ops, SparseCore 1:
  33.1 157.0 all-gather.1
where the time goes:
time: 891 us; the launch traced here: 888 us
  waiting for transfers between devices  417 us (47%)
  matrix products  141 us (16%)
  local copies, waits for them, and re-layouts  123 us (14%)
  blocking collectives  95.4 us (11%)
  other arithmetic  85 us (10%)
  between operations  15 us (2%)
  starting transfers between devices  11.2 us (1%)
    all_to_all x1, waiting for transfers between devices, on_device(): lax.all_to_all(joined, 'seq', split_axis=0, concat_axis=1, tiled=True)  223 us
    psum x1, waiting for transfers between devices, on_device(): lax.psum(up_terms, 'seq').astype(jnp.float32)  156 us
    all_to_all x1, blocking collectives, on_device(): lax.all_to_all(attended, 'seq', split_axis=1, concat_axis=0, tiled=True)  95.4 us
    dot_general x1, matrix products, on_device(): jnp.einsum('rtd,dc->rtc', block_rows, query_key_value_weight, preferred_e...  47.6 us
    all_to_all x1, waiting for transfers between devices, on_device(): lax.all_to_all(queries, 'seq', split_axis=0, concat_axis=1, tiled=True)  38.2 us
    dot_general x32, matrix products, one_block(): jnp.dot(weights.astype(jnp.bfloat16), value_rows, preferred_element_type=...  33.5 us
    dot_general x32, matrix products, one_block(): lax.dot_general(block_rows, key_rows, (((1,), (1,)), ((), ())), preferred...  29.7 us
    reduce_sum x32, other arithmetic, one_block(): weights = weights / jnp.sum(weights, axis=-1, keepdims=True)  27 us
  transfers between devices with their start and end apart: 4, of which 3 were waited for; matrix products, arithmetic and copies ran while one was open for 9% of the time, Pallas kernels for 0%

commit v1 on v0

--- a/solution.py
+++ b/solution.py
@@ -116,7 +116,10 @@
         lax.all_to_all(joined, "seq", split_axis=0, concat_axis=1, tiled=True),
     )
     attended = lax.map(attend_item, (query_items, joined_items))
-    returned = lax.all_to_all(attended, "seq", split_axis=1, concat_axis=0, tiled=True)
+    returned = jnp.concatenate(
+        lax.all_to_all(jnp.stack(jnp.split(attended, lax.axis_size("seq"), axis=1)), "seq", 0, 0),
+        axis=0,
+    )
     returned = returned.reshape(all_requests, heads_local, token_local, HEAD_SIZE)
     return jnp.transpose(returned, (0, 2, 1, 3)).reshape(
         all_requests, token_local, heads_local * HEAD_SIZE

time: 891 us -> 886 us (level)
  no operation moved by 1% of the time
where the time goes in v1:
time: 886 us; the launch traced here: 883 us
  waiting for transfers between devices  417 us (47%)
  matrix products  141 us (16%)
  local copies, waits for them, and re-layouts  117 us (13%)
  blocking collectives  95.4 us (11%)
  other arithmetic  85.6 us (10%)
  between operations  15 us (2%)
  starting transfers between devices  11.2 us (1%)
    all_to_all x1, waiting for transfers between devices, on_device(): lax.all_to_all(joined, 'seq', split_axis=0, concat_axis=1, tiled=True)  223 us
    psum x1, waiting for transfers between devices, on_device(): lax.psum(up_terms, 'seq').astype(jnp.float32)  156 us
    all_to_all x1, blocking collectives, on_device(): lax.all_to_all(jnp.stack(jnp.split(attended, lax.axis_size('seq'), axis=1...  95.4 us
    dot_general x1, matrix products, on_device(): jnp.einsum('rtd,dc->rtc', block_rows, query_key_value_weight, preferred_e...  47.6 us
    all_to_all x1, waiting for transfers between devices, on_device(): lax.all_to_all(queries, 'seq', split_axis=0, concat_axis=1, tiled=True)  38.2 us
    dot_general x32, matrix products, one_block(): jnp.dot(weights.astype(jnp.bfloat16), value_rows, preferred_element_type=...  33.5 us
    dot_general x32, matrix products, one_block(): lax.dot_general(block_rows, key_rows, (((1,), (1,)), ((), ())), preferred...  29.7 us
    reduce_sum x32, other arithmetic, one_block(): weights = weights / jnp.sum(weights, axis=-1, keepdims=True)  27 us
  transfers between devices with their start and end apart: 4, of which 3 were waited for; matrix products, arithmetic and copies ran while one was open for 9% of the time, Pallas kernels for 0%

profile of v1, /device:TPU:0, one launch (start us, length us, event | category | flops | bytes accessed | tf_op | source)
XLA Modules:
  0.0 883.0 jit_solution(18415514498255952773)
XLA Ops:
  9.2 2.8 convolution_convert_fusion
  12.1 3.1 convolution_convert_fusion.1
  15.2 3.7 convert_reduce_fusion
  18.9 4.5 fusion.10
  23.6 9.4 %fusion.13 = bf16[2,512,3072]{2,1,0:T(8,128)(2,1)} fusion(bf16[2,512,3072]{2,1,0:T(8,128)(2,1)} %param.14, f32[2,3072]{1,0:T(2,128)S(1)} %get-tuple-element.87, f32[2,512]{1,0:T(2,128)S(1)} %add_rsqrt_fusion.2, f32[2,512]{1,0:T(2,128)S(1)} %broadcast_multiply_fusion, f32[2,3072]{1,0:T(2,128)S(1)} %get-tuple-element.88), kind=kLoop, calls=%fused_computation.24 | loop fusion | flops 18874368 | bytes 12640256 | tf_op jit(solution)/shard_map/convert_element_type | solution.py:15
  34.2 156.1 %all-reduce.3.cloned.1.call-done = (bf16[8,64,1536]{2,0,1:T(8,128)(2,1)}, bf16[8,3072,64]{1,0,2:T(8,128)(2,1)}) async-done(((bf16[8,64,1536]{2,0,1:T(8,128)(2,1)}, bf16[8,3072,64]{1,0,2:T(8,128)(2,1)}), (bf16[8,64,1536]{2,0,1:T(8,128)(2,1)}, bf16[8,3072,64]{1,0,2:T(8,128)(2,1)})) %all-reduce.3.cloned.1.call-update) | async-done | bytes 4718608 | tf_op jit(solution)/shard_map/psum | solution.py:86
  190.3 23.9 %fusion.18 = f32[8,512,1536]{2,1,0:T(8,128)} fusion(bf16[8,64,1536]{2,0,1:T(8,128)(2,1)} %get-tuple-element.73, bf16[8,512,3072]{2,1,0:T(8,128)(2,1)} %all-gather.2.cloned.1.call-done, bf16[8,3072,64]{1,0,2:T(8,128)(2,1)} %get-tuple-element.74), kind=kOutput, calls=%fused_computation.42 | convolution fusion | flops 2416181248 | bytes 55050240 | tf_op jit(solution)/shard_map/rtk,rkc->rtc/dot_general | solution.py:97
  214.3 47.6 %convolution_add_fusion = f32[8,512,1536]{2,1,0:T(8,128)} fusion(f32[8,512,1536]{2,1,0:T(8,128)} %fusion.18, bf16[8,512,3072]{2,1,0:T(8,128)(2,1)} %all-gather.2.cloned.1.call-done, bf16[3072,1536]{1,0:T(8,128)(2,1)} %param.16), kind=kOutput, calls=%fused_computation.16 | convolution fusion | flops 38660997120 | bytes 84934656 | tf_op jit(solution)/shard_map/rtd,dc->rtc/dot_general | solution.py:94
  261.9 24.7 %copy.45 = f32[8,512,1536]{1,2,0:T(8,128)} copy(f32[8,512,1536]{2,1,0:T(8,128)} %convolution_add_fusion) | data formatting | bytes 50331648 | tf_op jit(solution)/shard_map/add | solution.py:97
  286.6 4.6 multiply_reduce_fusion.1
  291.2 7.0 fusion.15
  298.2 6.5 copy.46
  304.6 5.2 all-to-all-start
  309.8 6.2 copy.48
  316.0 3.2 copy.72
  319.1 4.0 slice.55
  323.1 4.6 multiply_reduce_fusion
  327.8 7.0 multiply_convert_fusion
  334.7 6.2 maximum_bitcast_fusion
  340.9 9.1 %pad_maximum_fusion = bf16[8,4,640,2,128]{2,4,3,1,0:T(8,128)(2,1)} fusion(bf16[8,4,128,2,128]{2,4,3,1,0:T(8,128)(2,1)} %bitcast.106, bf16[8,4,512,2,128]{2,4,3,1,0:T(8,128)(2,1)} %maximum_bitcast_fusion), kind=kLoop, calls=%fused_computation.25 | loop fusion | flops 20971520 | bytes 20971520 | tf_op jit(solution)/shard_map/concatenate | solution.py:109
  350.1 15.1 %copy.50 = bf16[8,4,640,2,128]{4,2,3,1,0:T(8,128)(2,1)} copy(bf16[8,4,640,2,128]{2,4,3,1,0:T(8,128)(2,1)} %pad_maximum_fusion) | data formatting | bytes 20971520 | tf_op jit(solution)/shard_map/concatenate | solution.py:109
  365.2 38.2 %all-to-all-done = bf16[32,512,128]{2,1,0:T(8,128)(2,1)} async-done(((bf16[32,512,128]{2,1,0:T(8,128)(2,1)}), bf16[32,512,128]{2,1,0:T(8,128)(2,1)}, u32[]{:S(2)}, u32[]{:S(2)}) %all-to-all-start) | async-done | bytes 4194336 | tf_op jit(solution)/shard_map/all_to_all | solution.py:115
  403.3 6.0 all-to-all-start.1
  409.4 4.6 copy.47
  414.0 223.2 %all-to-all-done.1 = bf16[32,640,2,128]{3,1,2,0:T(8,128)(2,1)} async-done(((bf16[32,640,2,128]{3,1,2,0:T(8,128)(2,1)}), bf16[32,640,2,128]{3,1,2,0:T(8,128)(2,1)}, u32[]{:S(2)}, u32[]{:S(2)}) %all-to-all-start.1) | async-done | bytes 10485792 | tf_op jit(solution)/shard_map/all_to_all | solution.py:116
  637.1 9.2 %copy.51 = bf16[8,4,640,2,128]{4,2,1,3,0:T(8,128)(2,1)} copy(bf16[8,4,640,2,128]{4,2,3,0,1:T(8,128)(2,1)} %bitcast.23) | data formatting | bytes 20971520 | tf_op jit(solution)/shard_map/all_to_all | solution.py:116
  646.3 118.3 %while.21 = (s32[]{:T(128)}, bf16[8,2048,128]{2,1,0:T(8,128)(2,1)}, bf16[8,2048,128]{2,1,0:T(8,128)(2,1)}, bf16[8,2560,2,128]{3,1,2,0:T(8,128)(2,1)}, s32[]{:T(128)}, /*index=5*/s32[]{:T(128)}, s32[]{:T(128)}) while((s32[]{:T(128)}, bf16[8,2048,128]{2,1,0:T(8,128)(2,1)}, bf16[8,2048,128]{2,1,0:T(8,128)(2,1)}, ...), condition=%wide.region_13.14_spmd, body=%wide.region_8.13_spmd.sunk | while | flops 680328192 | bytes 24652504 | solution.py:118
  646.3 1.4 dynamic-slice_bitcast_fusion.2
  648.9 11.3 %while.22 = (s32[]{:T(128)}, bf16[4,512,128]{2,1,0:T(8,128)(2,1)S(1)}, bf16[4,512,128]{2,1,0:T(8,128)(2,1)S(1)}, bf16[2560,128]{1,0:T(8,128)(2,1)S(1)}, bf16[2560,128]{1,0:T(8,128)(2,1)S(1)}, /*index=5*/s32[]{:T(128)}) while((s32[]{:T(128)}, bf16[4,512,128]{2,1,0:T(8,128)(2,1)S(1)}, bf16[4,512,128]{2,1,0:T(8,128)(2,1)S(1)}, ...), condition=%wide.region_12.12_spmd, body=%wide.region_9.11_spmd.sunk | while | flops 680328192 | bytes 17311820 | solution.py:47
  661.1 1.4 dynamic-slice_bitcast_fusion.2
  663.7 11.4 %while.22 = (s32[]{:T(128)}, bf16[4,512,128]{2,1,0:T(8,128)(2,1)S(1)}, bf16[4,512,128]{2,1,0:T(8,128)(2,1)S(1)}, bf16[2560,128]{1,0:T(8,128)(2,1)S(1)}, bf16[2560,128]{1,0:T(8,128)(2,1)S(1)}, /*index=5*/s32[]{:T(128)}) while((s32[]{:T(128)}, bf16[4,512,128]{2,1,0:T(8,128)(2,1)S(1)}, bf16[4,512,128]{2,1,0:T(8,128)(2,1)S(1)}, ...), condition=%wide.region_12.12_spmd, body=%wide.region_9.11_spmd.sunk | while | flops 680328192 | bytes 17311820 | solution.py:47
  675.9 1.4 dynamic-slice_bitcast_fusion.2
  677.4 1.1 constant_dynamic-slice_fusion.2
  678.5 11.4 %while.22 = (s32[]{:T(128)}, bf16[4,512,128]{2,1,0:T(8,128)(2,1)S(1)}, bf16[4,512,128]{2,1,0:T(8,128)(2,1)S(1)}, bf16[2560,128]{1,0:T(8,128)(2,1)S(1)}, bf16[2560,128]{1,0:T(8,128)(2,1)S(1)}, /*index=5*/s32[]{:T(128)}) while((s32[]{:T(128)}, bf16[4,512,128]{2,1,0:T(8,128)(2,1)S(1)}, bf16[4,512,128]{2,1,0:T(8,128)(2,1)S(1)}, ...), condition=%wide.region_12.12_spmd, body=%wide.region_9.11_spmd.sunk | while | flops 680328192 | bytes 17311820 | solution.py:47
  690.7 1.4 dynamic-slice_bitcast_fusion.2
  693.3 11.4 %while.22 = (s32[]{:T(128)}, bf16[4,512,128]{2,1,0:T(8,128)(2,1)S(1)}, bf16[4,512,128]{2,1,0:T(8,128)(2,1)S(1)}, bf16[2560,128]{1,0:T(8,128)(2,1)S(1)}, bf16[2560,128]{1,0:T(8,128)(2,1)S(1)}, /*index=5*/s32[]{:T(128)}) while((s32[]{:T(128)}, bf16[4,512,128]{2,1,0:T(8,128)(2,1)S(1)}, bf16[4,512,128]{2,1,0:T(8,128)(2,1)S(1)}, ...), condition=%wide.region_12.12_spmd, body=%wide.region_9.11_spmd.sunk | while | flops 680328192 | bytes 17311820 | solution.py:47
  705.5 1.4 dynamic-slice_bitcast_fusion.2
  708.1 11.4 %while.22 = (s32[]{:T(128)}, bf16[4,512,128]{2,1,0:T(8,128)(2,1)S(1)}, bf16[4,512,128]{2,1,0:T(8,128)(2,1)S(1)}, bf16[2560,128]{1,0:T(8,128)(2,1)S(1)}, bf16[2560,128]{1,0:T(8,128)(2,1)S(1)}, /*index=5*/s32[]{:T(128)}) while((s32[]{:T(128)}, bf16[4,512,128]{2,1,0:T(8,128)(2,1)S(1)}, bf16[4,512,128]{2,1,0:T(8,128)(2,1)S(1)}, ...), condition=%wide.region_12.12_spmd, body=%wide.region_9.11_spmd.sunk | while | flops 680328192 | bytes 17311820 | solution.py:47
  720.3 1.4 dynamic-slice_bitcast_fusion.2
  722.9 11.4 %while.22 = (s32[]{:T(128)}, bf16[4,512,128]{2,1,0:T(8,128)(2,1)S(1)}, bf16[4,512,128]{2,1,0:T(8,128)(2,1)S(1)}, bf16[2560,128]{1,0:T(8,128)(2,1)S(1)}, bf16[2560,128]{1,0:T(8,128)(2,1)S(1)}, /*index=5*/s32[]{:T(128)}) while((s32[]{:T(128)}, bf16[4,512,128]{2,1,0:T(8,128)(2,1)S(1)}, bf16[4,512,128]{2,1,0:T(8,128)(2,1)S(1)}, ...), condition=%wide.region_12.12_spmd, body=%wide.region_9.11_spmd.sunk | while | flops 680328192 | bytes 17311820 | solution.py:47
  735.1 1.4 dynamic-slice_bitcast_fusion.2
  737.6 11.4 %while.22 = (s32[]{:T(128)}, bf16[4,512,128]{2,1,0:T(8,128)(2,1)S(1)}, bf16[4,512,128]{2,1,0:T(8,128)(2,1)S(1)}, bf16[2560,128]{1,0:T(8,128)(2,1)S(1)}, bf16[2560,128]{1,0:T(8,128)(2,1)S(1)}, /*index=5*/s32[]{:T(128)}) while((s32[]{:T(128)}, bf16[4,512,128]{2,1,0:T(8,128)(2,1)S(1)}, bf16[4,512,128]{2,1,0:T(8,128)(2,1)S(1)}, ...), condition=%wide.region_12.12_spmd, body=%wide.region_9.11_spmd.sunk | while | flops 680328192 | bytes 17311820 | solution.py:47
  749.8 1.4 dynamic-slice_bitcast_fusion.2
  752.4 11.4 %while.22 = (s32[]{:T(128)}, bf16[4,512,128]{2,1,0:T(8,128)(2,1)S(1)}, bf16[4,512,128]{2,1,0:T(8,128)(2,1)S(1)}, bf16[2560,128]{1,0:T(8,128)(2,1)S(1)}, bf16[2560,128]{1,0:T(8,128)(2,1)S(1)}, /*index=5*/s32[]{:T(128)}) while((s32[]{:T(128)}, bf16[4,512,128]{2,1,0:T(8,128)(2,1)S(1)}, bf16[4,512,128]{2,1,0:T(8,128)(2,1)S(1)}, ...), condition=%wide.region_12.12_spmd, body=%wide.region_9.11_spmd.sunk | while | flops 680328192 | bytes 17311820 | solution.py:47
  764.6 2.6 slice_bitcast_fusion.6
  767.8 95.4 %all_to_all.41 = bf16[4,8,512,128]{3,2,1,0:T(8,128)(2,1)S(1)} all-to-all(bf16[4,8,512,128]{3,2,1,0:T(8,128)(2,1)S(1)} %pad_maximum_fusion.1), channel_id=1, replica_groups=mesh['groups'=2,'seq'=4,'adapt'=4] {'seq'}, dimensions={0} | all-to-all | bytes 8388608 | tf_op jit(solution)/shard_map/all_to_all | solution.py:120
  863.2 5.2 copy.71
  868.4 7.2 reshape.93
  (155 shorter events, 109.0 us)
Async XLA Ops:
  7.4 1.8 copy-start
  7.4 182.9 %all-reduce.3.cloned.1.call-start = ((), (), s32[]{:S(2)}) async-start(), calls=%async_computation.4 | async-start | bytes 9437184 | tf_op jit(solution)/shard_map/psum | solution.py:86
  15.2 8.3 copy-start.2
  15.2 175.1 %all-gather.2.cloned.1.call-start = ((), (), s32[]{:S(2)}) async-start(), calls=%async_computation.3 | async-start | bytes 31457280 | tf_op jit(solution)/shard_map/all_gather | solution.py:90
  33.0 0.7 copy-start.4
  304.6 98.7 %all-to-all-start = ((bf16[32,512,128]{2,1,0:T(8,128)(2,1)}), bf16[32,512,128]{2,1,0:T(8,128)(2,1)}, u32[]{:S(2)}, u32[]{:S(2)}) async-start(bf16[32,512,128]{2,1,0:T(8,128)(2,1)} %bitcast.101), calls=%async_computation | async-start | bytes 8388608 | tf_op jit(solution)/shard_map/all_to_all | solution.py:115
  323.1 4.6 copy-start.3
  403.3 233.8 %all-to-all-start.1 = ((bf16[32,640,2,128]{3,1,2,0:T(8,128)(2,1)}), bf16[32,640,2,128]{3,1,2,0:T(8,128)(2,1)}, u32[]{:S(2)}, u32[]{:S(2)}) async-start(bf16[32,640,2,128]{3,1,2,0:T(8,128)(2,1)} %bitcast.99), calls=%async_computation.1 | async-start | bytes 20971520 | tf_op jit(solution)/shard_map/all_to_all | solution.py:116
  863.2 12.3 %copy-start.1 = (bf16[4,3072,64]{1,2,0:T(8,128)(2,1)S(1)}, bf16[4,3072,64]{1,2,0:T(8,128)(2,1)}, u32[]{:S(2)}) copy-start(bf16[4,3072,64]{1,2,0:T(8,128)(2,1)} %param.17) | copy-start | bytes 4718596
Sparse Core Ops, SparseCore 0:
  15.3 174.9 all-reduce.2
Sparse Core Ops, SparseCore 1:
  33.1 157.0 all-gather.1
